TPU v7x, 256 devices: a whole 4x4x8 slice. The times are simulated.
256 devices in a mesh: grp: 64 (over z, y, core), head: 4 (over x).
Axes of the slice: x: 4, y: 4, z: 8, core: 2. Of those that a mesh axis runs over, the one named last changes fastest.
Arguments:
- arriving_hiddens: bfloat16 [512, 4, 2048], P('grp', None, 'head'), may hold values from -6 to 6
- occupied_slot_totals: int32 [512], P('grp'), may hold values from 1 to 4
- former_indices: int32 [512], P('grp'), may hold values from 0 to 511, as said below
- reconstruct_marks: int32 [512], P('grp'), may hold values from 0 to 1, as said below
- retained_hiddens: bfloat16 [512, 32, 2048], P('grp', None, 'head'), may hold values from -6 to 6
- carried_memory_matrices: float32 [512, 16, 64, 64], P('grp', 'head'), may hold values from -12 to 12
- lagged_previous_entries: float32 [512, 2, 2048], P('grp', None, 'head'), may hold values from -6 to 6
- pre_attention_scaling: float32 [2048], replicated, may hold values from 0.5 to 1.5
- pre_feedforward_scaling: float32 [2048], replicated, may hold values from 0.5 to 1.5
- lag_blend_fractions: float32 [5, 2048], replicated, may hold values from 0 to 1
- acceptance_projection: bfloat16 [2048, 1024], P(None, 'head'), may hold values from -0.125 to 0.125
- address_projection: bfloat16 [2048, 1024], P(None, 'head'), may hold values from -0.125 to 0.125
- content_projection: bfloat16 [2048, 1024], P(None, 'head'), may hold values from -0.125 to 0.125
- fading_lowrank_left: bfloat16 [2048, 64], replicated, may hold values from -0.125 to 0.125
- fading_lowrank_right: bfloat16 [64, 1024], P(None, 'head'), may hold values from -0.75 to 0.75
- fading_baseline_entries: float32 [1024], P('head'), may hold values from -6 to 1
- present_item_reward: float32 [1024], P('head'), may hold values from -6 to 6
- grouped_layer_scaling: float32 [1024], P('head'), may hold values from 0.5 to 1.5
- attention_exit_projection: bfloat16 [1024, 2048], P('head'), may hold values from -0.1875 to 0.1875
- feedforward_address_proj: bfloat16 [2048, 3584], P(None, 'head'), may hold values from -0.125 to 0.125
- feedforward_content_proj: bfloat16 [3584, 2048], P('head'), may hold values from -0.09375 to 0.09375
Outputs:
- next_tokens: bfloat16 [512, 4, 2048], P('grp', None, 'head')
- next_state: float32 [512, 16, 64, 64], P('grp', 'head')
- next_shift: float32 [512, 2, 2048], P('grp', None, 'head')
Inputs may be any that keep to these rules, and one draw needn't show every extreme that they name: former_indices[g * 8 + j] = ((g + offset_j) mod 64) * 8 + local_j, where the 8 offsets offset_j are distinct numbers of 0 to 63 and local_j is a permutation of 0 to 7, both the same for every group g. `reconstruct_marks`: among the 8 requests of one group at most 2 are marked, and some group has exactly 2.
All inputs are finite; a program needn't handle non-finite values.
Results may differ from a plain program's by a relative error of at most 0.028.
Values may be sent and summed in bfloat16 or wider, within the bound.
No kernel may reach another device: no remote copies, remote signals or barrier semaphores. Data moves between devices by JAX's collectives and lax.ppermute only.
A program may use at most 128 MiB of HBM per device.

v0:
```python
import jax
import jax.numpy as jnp
from jax import lax
from jax.sharding import PartitionSpec as P

ATTENTION_WIDTH = 64
REB = 2
EPSILON = 1e-05


def shifted_2(value, axis, steps):
    count = lax.axis_size(axis)
    pairs = [(source, (source + steps) % count) for source in range(count)]
    return lax.ppermute(value, axis, pairs)


def layer_norm(inputs, gain):
    centered = inputs - jnp.mean(inputs, axis=-1, keepdims=True)
    spread = jnp.mean(centered * centered, axis=-1, keepdims=True)
    return (centered * lax.rsqrt(spread + EPSILON) * gain).astype(jnp.bfloat16)


def blend_rows(current, previous, rate):
    return (current + (previous - current) * rate).astype(jnp.bfloat16)


def project(inputs, weight):
    flat_rows = inputs.reshape(-1, inputs.shape[-1])
    result = jnp.dot(flat_rows, weight, preferred_element_type=jnp.float32)
    return result.reshape(inputs.shape[:-1] + (weight.shape[1],))


def divide_into_groups(inputs):
    return inputs.reshape(inputs.shape[:-1] + (-1, ATTENTION_WIDTH))


def key_value_decay(
    current,
    previous,
    lag_blend_fractions,
    address_projection,
    content_projection,
    fading_lowrank_left,
    fading_lowrank_right,
    fading_baseline_entries,
):
    key_rows = project(blend_rows(current, previous, lag_blend_fractions[1]), address_projection)
    values = project(blend_rows(current, previous, lag_blend_fractions[2]), content_projection)
    lowrank = jnp.tanh(
        project(blend_rows(current, previous, lag_blend_fractions[3]), fading_lowrank_left)
    ).astype(jnp.bfloat16)
    decay_rates = jnp.exp(
        -jnp.exp(fading_baseline_entries + project(lowrank, fading_lowrank_right))
    )
    return (
        divide_into_groups(key_rows),
        divide_into_groups(values),
        divide_into_groups(decay_rates),
    )


def advance(present_outer_product, inputs):
    key_step, value_step, decay_step = inputs
    return (
        decay_step[..., :, None] * present_outer_product
        + key_step[..., :, None] * value_step[..., None, :],
        None,
    )


def rebuild(
    retained_hiddens,
    pre_attention_scaling,
    lag_blend_fractions,
    address_projection,
    content_projection,
    fading_lowrank_left,
    fading_lowrank_right,
    fading_baseline_entries,
):
    standardized_entry = layer_norm(retained_hiddens.astype(jnp.float32), pre_attention_scaling)
    current = standardized_entry.astype(jnp.float32)
    previous = jnp.concatenate([jnp.zeros_like(current[:, :1]), current[:, :-1]], axis=1)
    key_rows, values, decay_rates = key_value_decay(
        current,
        previous,
        lag_blend_fractions,
        address_projection,
        content_projection,
        fading_lowrank_left,
        fading_lowrank_right,
        fading_baseline_entries,
    )
    start_state = jnp.zeros(
        key_rows.shape[:1] + key_rows.shape[2:] + (ATTENTION_WIDTH,), jnp.float32
    )
    final_state, _ = lax.scan(
        advance,
        start_state,
        (jnp.moveaxis(key_rows, 1, 0), jnp.moveaxis(values, 1, 0), jnp.moveaxis(decay_rates, 1, 0)),
    )
    return (final_state, current[:, -1])


def attention_result(
    standardized_entry,
    lagged_entry,
    present_outer_product,
    occupied_slot_totals,
    lag_blend_fractions,
    acceptance_projection,
    address_projection,
    content_projection,
    fading_lowrank_left,
    fading_lowrank_right,
    fading_baseline_entries,
    present_item_reward,
    grouped_layer_scaling,
):
    current = standardized_entry.astype(jnp.float32)
    previous = jnp.concatenate([lagged_entry[:, None], current[:, :-1]], axis=1)
    acceptance_gate_entries = divide_into_groups(
        project(blend_rows(current, previous, lag_blend_fractions[0]), acceptance_projection)
    )
    key_rows, values, decay_rates = key_value_decay(
        current,
        previous,
        lag_blend_fractions,
        address_projection,
        content_projection,
        fading_lowrank_left,
        fading_lowrank_right,
        fading_baseline_entries,
    )
    reward_grouped = divide_into_groups(present_item_reward)
    decoding_results = []
    for query_slot_index in range(current.shape[1]):
        address_content_product = (
            key_rows[:, query_slot_index, :, :, None] * values[:, query_slot_index, :, None, :]
        )
        decoding_results.append(
            jnp.einsum(
                "ghl,ghlm->ghm",
                acceptance_gate_entries[:, query_slot_index],
                present_outer_product + reward_grouped[:, :, None] * address_content_product,
                precision=lax.Precision.HIGHEST,
            )
        )
        valid_rows = (query_slot_index < occupied_slot_totals)[:, None, None, None]
        present_outer_product = jnp.where(
            valid_rows,
            decay_rates[:, query_slot_index, :, :, None] * present_outer_product
            + address_content_product,
            present_outer_product,
        )
    mixed_heads = jnp.stack(decoding_results, axis=1)
    centered = mixed_heads - jnp.mean(mixed_heads, axis=-1, keepdims=True)
    spread = jnp.mean(centered * centered, axis=-1, keepdims=True)
    grouped_results = (
        centered * lax.rsqrt(spread + EPSILON) * divide_into_groups(grouped_layer_scaling)
    ).astype(jnp.bfloat16)
    return (grouped_results.reshape(grouped_results.shape[:2] + (-1,)), present_outer_product)


def last_live(inputs, occupied_slot_totals):
    pick_table = (
        jnp.arange(inputs.shape[1])[None, :, None] == (occupied_slot_totals - 1)[:, None, None]
    )
    return jnp.sum(jnp.where(pick_table, inputs, jnp.zeros_like(inputs)), axis=1)


def on_device(
    arriving_hiddens,
    occupied_slot_totals,
    former_indices,
    reconstruct_marks,
    retained_hiddens,
    carried_memory_matrices,
    lagged_previous_entries,
    pre_attention_scaling,
    pre_feedforward_scaling,
    lag_blend_fractions,
    acceptance_projection,
    address_projection,
    content_projection,
    fading_lowrank_left,
    fading_lowrank_right,
    fading_baseline_entries,
    present_item_reward,
    grouped_layer_scaling,
    attention_exit_projection,
    feedforward_address_proj,
    feedforward_content_proj,
):
    req_rows = arriving_hiddens.shape[0]
    local_heads = carried_memory_matrices.shape[1]
    model_width = pre_attention_scaling.shape[0]
    grp_index = lax.axis_index("grp")
    groups = lax.axis_size("grp")
    head_index = lax.axis_index("head")
    feature_part = model_width // lax.axis_size("head")
    offset = (former_indices // req_rows - grp_index) % groups
    source_row = former_indices % req_rows
    state_size = local_heads * ATTENTION_WIDTH * ATTENTION_WIDTH
    packed = jnp.concatenate(
        [
            carried_memory_matrices.reshape(req_rows, -1),
            lagged_previous_entries.reshape(req_rows, -1),
        ],
        axis=1,
    )
    ready_rows = jnp.take(packed, source_row, axis=0)
    moved_rows = ready_rows
    for bit_index in range((groups - 1).bit_length()):
        shifted = shifted_2(moved_rows, "grp", -(1 << bit_index))
        moved_rows = jnp.where((offset >> bit_index & 1 == 1)[:, None], shifted, moved_rows)
    present_outer_product = moved_rows[:, :state_size].reshape(
        req_rows, local_heads, ATTENTION_WIDTH, ATTENTION_WIDTH
    )
    shift_part = moved_rows[:, state_size:].reshape(req_rows, 2, feature_part)
    mark_rank = jnp.cumsum(reconstruct_marks) - reconstruct_marks
    slot_table = (
        (reconstruct_marks[None, :] == 1) & (mark_rank[None, :] == jnp.arange(REB)[:, None])
    ).astype(jnp.bfloat16)
    chosen = jnp.einsum(
        "sn,ntd->std", slot_table, retained_hiddens, preferred_element_type=jnp.float32
    ).astype(jnp.bfloat16)
    full_tokens, full_chosen = (
        lax.all_gather(arriving_hiddens, "head", axis=2, tiled=True),
        lax.all_gather(chosen, "head", axis=2, tiled=True),
    )
    full_shift = lax.all_gather(shift_part.astype(jnp.bfloat16), "head", axis=2, tiled=True).astype(
        shift_part.dtype
    )
    rebuilt, last_hist = rebuild(
        full_chosen,
        pre_attention_scaling,
        lag_blend_fractions,
        address_projection,
        content_projection,
        fading_lowrank_left,
        fading_lowrank_right,
        fading_baseline_entries,
    )
    pick_slot = jnp.clip(mark_rank, 0, REB - 1)
    marked = reconstruct_marks == 1
    present_outer_product = jnp.where(
        marked[:, None, None, None], jnp.take(rebuilt, pick_slot, axis=0), present_outer_product
    )
    lagged_entry = jnp.where(
        marked[:, None], jnp.take(last_hist, pick_slot, axis=0), full_shift[:, 0]
    )
    standardized_entry = layer_norm(full_tokens.astype(jnp.float32), pre_attention_scaling)
    grouped_results, present_outer_product = attention_result(
        standardized_entry,
        lagged_entry,
        present_outer_product,
        occupied_slot_totals,
        lag_blend_fractions,
        acceptance_projection,
        address_projection,
        content_projection,
        fading_lowrank_left,
        fading_lowrank_right,
        fading_baseline_entries,
        present_item_reward,
        grouped_layer_scaling,
    )
    flat_heads = grouped_results.reshape(-1, grouped_results.shape[-1])
    mix_total = lax.psum(
        jnp.dot(flat_heads, attention_exit_projection, preferred_element_type=jnp.float32).astype(
            jnp.bfloat16
        ),
        "head",
    ).astype(jnp.float32)
    middle = (full_tokens.astype(jnp.float32) + mix_total.reshape(full_tokens.shape)).astype(
        jnp.bfloat16
    )
    middle_local = lax.dynamic_slice_in_dim(middle, head_index * feature_part, feature_part, 2)
    second = layer_norm(middle.astype(jnp.float32), pre_feedforward_scaling)
    current = second.astype(jnp.float32)
    previous = jnp.concatenate([full_shift[:, 1][:, None], current[:, :-1]], axis=1)
    hidden = jnp.square(
        jax.nn.relu(
            project(blend_rows(current, previous, lag_blend_fractions[4]), feedforward_address_proj)
        )
    ).astype(jnp.bfloat16)
    flat_hidden = hidden.reshape(-1, hidden.shape[-1])
    ffn_rows = lax.psum_scatter(
        lax.dot_general(
            feedforward_content_proj,
            flat_hidden,
            (((0,), (1,)), ((), ())),
            preferred_element_type=jnp.float32,
        ).astype(jnp.bfloat16),
        "head",
        scatter_dimension=0,
        tiled=True,
    ).astype(jnp.float32)
    result = (middle_local.astype(jnp.float32) + ffn_rows.T.reshape(middle_local.shape)).astype(
        jnp.bfloat16
    )
    valid_rows = jnp.arange(arriving_hiddens.shape[1])[None, :] < occupied_slot_totals[:, None]
    result = jnp.where(valid_rows[..., None], result, jnp.zeros_like(result))
    time_last = lax.dynamic_slice_in_dim(
        last_live(standardized_entry.astype(jnp.float32), occupied_slot_totals),
        head_index * feature_part,
        feature_part,
        1,
    )
    channel_last = lax.dynamic_slice_in_dim(
        last_live(current, occupied_slot_totals), head_index * feature_part, feature_part, 1
    )
    return (result, present_outer_product, jnp.stack([time_last, channel_last], axis=1))


def solution(mesh):
    placed = (
        P("grp", None, "head"),
        P("grp"),
        P("grp"),
        P("grp"),
        P("grp", None, "head"),
        P("grp", "head", None, None),
        P("grp", None, "head"),
        P(),
        P(),
        P(),
        P(None, "head"),
        P(None, "head"),
        P(None, "head"),
        P(),
        P(None, "head"),
        P("head"),
        P("head"),
        P("head"),
        P("head", None),
        P(None, "head"),
        P("head", None),
    )
    return jax.shard_map(
        on_device,
        mesh=mesh,
        in_specs=placed,
        out_specs=(P("grp", None, "head"), P("grp", "head", None, None), P("grp", None, "head")),
        check_vma=False,
    )
```

profile of v0, /device:TPU:8, one launch (start us, length us, event | category | flops | bytes accessed | tf_op | source)
XLA Modules:
  0.0 305.9 jit_solution(17810951148594460560)
XLA Ops:
  15.0 12.6 %all_gather.10 = bf16[2,32,2048]{2,1,0:T(8,128)(2,1)S(1)} all-gather(bf16[2,32,512]{2,1,0:T(8,128)(2,1)S(1)} %copy.145), channel_id=1, replica_groups=mesh['grp'=64,'head'=4] {'head'}, dimensions={2}, use_global_device_ids=true | all-gather | bytes 327680 | tf_op jit(solution)/shard_map/all_gather | solution.py:230
  30.2 8.3 %collective-permute-start.1 = (f32[8,17408]{1,0:T(8,128)S(1)}, f32[8,17408]{1,0:T(8,128)}, u32[]{:S(2)}, u32[]{:S(2)}) collective-permute-start(f32[8,17408]{1,0:T(8,128)S(1)} %broadcast_select_fusion.1), channel_id=1, source_target_pairs={{0,248},{4,252},{8,0},{12,4},{16,8},{20,12},{24,16},{28,20},{32,24... | collective-permute-start | bytes 1671176 | tf_op jit(solution)/shard_map/ppermute | solution.py:14
  40.1 2.3 copy.80
  43.9 2.4 convolution_bitcast_fusion.1
  46.3 2.4 convolution_bitcast_fusion
  50.0 5.3 %collective-permute-start.2 = (f32[8,17408]{1,0:T(8,128)S(1)}, f32[8,17408]{1,0:T(8,128)}, u32[]{:S(2)}, u32[]{:S(2)}) collective-permute-start(f32[8,17408]{1,0:T(8,128)S(1)} %broadcast_select_fusion.2), channel_id=1, source_target_pairs={{0,240},{4,244},{8,248},{12,252},{16,0},{20,4},{24,8},{28,12},{32,... | collective-permute-start | bytes 1671176 | tf_op jit(solution)/shard_map/ppermute | solution.py:14
  55.4 34.7 %while.11 = (s32[]{:T(128)}, f32[2,4,64,64]{3,2,1,0:T(8,128)S(1)}, f32[32,2,4,64]{3,2,1,0:T(4,128)S(1)}, f32[32,2,4,64]{3,0,2,1:T(8,128)S(1)}, f32[32,2,4,64]{3,0,2,1:T(8,128)}, /*index=5*/s32[]{:T(128)}, s32[]{:T(128)}) while((s32[]{:T(128)}, f32[2,4,64,64]{3,2,1,0:T(8,128)S(1)}, f32[32,2,4,64]{3,2,1,0:T(4,128)S(1)}, ...), condition=%wide.region_6.7_spmd.clone, body=%wide.region_5.6_spmd.clone.sunk | while | flops 131075 | bytes 280679 | solution.py:97
  92.4 2.3 copy.77
  94.7 12.0 %all_gather.9 = bf16[8,4,2048]{2,1,0:T(4,128)(2,1)S(1)} all-gather(bf16[8,4,512]{2,1,0:T(4,128)(2,1)S(1)} %copy-done.16), channel_id=1, replica_groups=mesh['grp'=64,'head'=4] {'head'}, dimensions={2}, use_global_device_ids=true | all-gather | bytes 163840 | tf_op jit(solution)/shard_map/all_gather | solution.py:229
  108.7 18.3 %collective-permute-done.3 = f32[8,17408]{1,0:T(8,128)S(1)} collective-permute-done((f32[8,17408]{1,0:T(8,128)S(1)}, f32[8,17408]{1,0:T(8,128)S(1)}, u32[]{:S(2)}, u32[]{:S(2)}) %collective-permute-start.3) | collective-permute-done | bytes 557088 | tf_op jit(solution)/shard_map/ppermute | solution.py:14
  128.1 38.4 %collective-permute-done.4 = f32[8,17408]{1,0:T(8,128)S(1)} collective-permute-done((f32[8,17408]{1,0:T(8,128)S(1)}, f32[8,17408]{1,0:T(8,128)S(1)}, u32[]{:S(2)}, u32[]{:S(2)}) %collective-permute-start.4) | collective-permute-done | bytes 557088 | tf_op jit(solution)/shard_map/ppermute | solution.py:14
  168.1 18.2 %collective-permute-done.5 = f32[8,17408]{1,0:T(8,128)} collective-permute-done((f32[8,17408]{1,0:T(8,128)S(1)}, f32[8,17408]{1,0:T(8,128)}, u32[]{:S(2)}, u32[]{:S(2)}) %collective-permute-start.5) | collective-permute-done | bytes 557088 | tf_op jit(solution)/shard_map/ppermute | solution.py:14
  188.4 12.0 %all_gather.11 = bf16[8,2,2048]{2,0,1:T(8,128)(2,1)S(1)} all-gather(bf16[8,2,512]{2,0,1:T(8,128)(2,1)S(1)} %bitcast.193), channel_id=1, replica_groups=mesh['grp'=64,'head'=4] {'head'}, dimensions={2}, use_global_device_ids=true | all-gather | bytes 81920 | tf_op jit(solution)/shard_map/all_gather | solution.py:232
  205.2 1.9 fusion.105
  207.1 1.9 fusion.103
  209.1 1.8 fusion.101
  211.0 4.1 %fusion.36 = (f32[8,4,64,64]{3,2,1,0:T(8,128)}, f32[8,4,64,64]{3,2,1,0:T(8,128)S(1)}) fusion(f32[8,4,64]{2,1,0:T(4,128)S(1)} %copy-done.13, f32[8,4,64]{2,1,0:T(4,128)S(1)} %copy.94, f32[8,4,64]{2,1,0:T(4,128)S(1)} %copy.93, f32[8,4,64]{2,1,0:T(4,128)S(1)} %copy-done.12, f32[8,4,64]{2,1,0:T(4,128)S(1)} %copy.92, f32[8,4,64]{2,1,0:T(4,128)S(1)} %copy.91, ...), kind=kLoop, calls=%fused_computation.49 | loop fusion | flops 2359296 | bytes 2195504 | tf_op jit(solution)/shard_map/jit(_where)/select_n | solution.py:150
  215.2 2.8 fusion.34
  218.0 2.3 fusion.30
  220.3 1.7 fusion.26
  225.3 40.4 %all-reduce.3.cloned.1.call-done = bf16[8,4,2048]{2,1,0:T(4,128)(2,1)} async-done(((bf16[8,4,2048]{2,1,0:T(4,128)(2,1)}), bf16[8,4,2048]{2,1,0:T(4,128)(2,1)}) %all-reduce.3.cloned.1.call-update) | async-done | bytes 131088 | tf_op jit(solution)/shard_map/psum | solution.py:270
  267.8 2.7 fusion.10
  270.6 3.4 %fusion.3 = bf16[2048,32]{0,1:T(8,128)(2,1)} fusion(bf16[32,896]{1,0:T(8,128)(2,1)S(1)} %reshape.296, bf16[896,2048]{1,0:T(8,128)(2,1)} %param.43), kind=kOutput, calls=%fused_computation.12 | convolution fusion | flops 117506048 | bytes 3858432 | tf_op jit(solution)/shard_map/dot_general | solution.py:290
  274.7 22.9 %reduce-scatter.2.cloned.1.call-done = bf16[512,32]{0,1:T(8,128)(2,1)} async-done(((bf16[2048,32]{0,1:T(8,128)(2,1)}), bf16[512,32]{0,1:T(8,128)(2,1)}) %reduce-scatter.2.cloned.1.call-update) | async-done | bytes 32784 | tf_op jit(solution)/shard_map/reduce_scatter | solution.py:289
  (274 shorter events, 69.7 us)
Async XLA Ops:
  7.2 216.6 %copy-start = (bf16[256,2048]{1,0:T(8,128)(2,1)S(1)}, bf16[256,2048]{1,0:T(8,128)(2,1)}, u32[]{:S(2)}) copy-start(bf16[256,2048]{1,0:T(8,128)(2,1)} %param.41) | copy-start | bytes 3145732
  7.2 258.5 %all-reduce.3.cloned.1.call-start = ((), (), s32[]{:S(2)}) async-start(), calls=%async_computation.1 | async-start | bytes 262144 | tf_op jit(solution)/shard_map/psum | solution.py:270
  11.8 26.7 %copy-start.17 = (bf16[64,256]{1,0:T(8,128)(2,1)S(1)}, bf16[64,256]{1,0:T(8,128)(2,1)}, u32[]{:S(2)}) copy-start(bf16[64,256]{1,0:T(8,128)(2,1)} %param.37) | copy-start | bytes 98308
  11.8 26.7 %copy-start.30 = (f32[256]{0:T(256)S(1)}, f32[256]{0:T(256)}, u32[]{:S(2)}) copy-start(f32[256]{0:T(256)} %param.38) | copy-start | bytes 3076
  12.7 15.4 %collective-permute-start = (f32[8,17408]{1,0:T(8,128)}, f32[8,17408]{1,0:T(8,128)S(1)}, u32[]{:S(2)}, u32[]{:S(2)}) collective-permute-start(f32[8,17408]{1,0:T(8,128)} %broadcast_select_fusion), channel_id=1, source_target_pairs={{0,252},{4,0},{8,4},{12,8},{16,12},{20,16},{24,20},{28,24},{32,28}... | collective-permute-start | bytes 1671176 | tf_op jit(solution)/shard_map/ppermute | solution.py:14
  13.5 187.6 %copy-start.19 = (pred[8]{0:T(512)(128)(4,1)}, pred[8]{0:T(512)(128)(4,1)S(1)}, u32[]{:S(2)}) copy-start(pred[8]{0:T(512)(128)(4,1)S(1)} %get-tuple-element.124) | copy-start | bytes 28
  30.2 18.5 %collective-permute-start.1 = (f32[8,17408]{1,0:T(8,128)S(1)}, f32[8,17408]{1,0:T(8,128)}, u32[]{:S(2)}, u32[]{:S(2)}) collective-permute-start(f32[8,17408]{1,0:T(8,128)S(1)} %broadcast_select_fusion.1), channel_id=1, source_target_pairs={{0,248},{4,252},{8,0},{12,4},{16,8},{20,12},{24,16},{28,20},{32,24... | collective-permute-start | bytes 1671176 | tf_op jit(solution)/shard_map/ppermute | solution.py:14
  48.7 46.0 %copy-start.16 = (bf16[8,4,512]{2,1,0:T(4,128)(2,1)S(1)}, bf16[8,4,512]{2,1,0:T(4,128)(2,1)}, u32[]{:S(2)}) copy-start(bf16[8,4,512]{2,1,0:T(4,128)(2,1)} %param.23) | copy-start | bytes 98308
  50.0 58.1 %copy-start.35 = (s32[8]{0:T(128)S(1)}, s32[8]{0:T(128)}, u32[]{:S(2)}) copy-start(s32[8]{0:T(128)} %param.24) | copy-start | bytes 100
  50.0 56.6 %collective-permute-start.2 = (f32[8,17408]{1,0:T(8,128)S(1)}, f32[8,17408]{1,0:T(8,128)}, u32[]{:S(2)}, u32[]{:S(2)}) collective-permute-start(f32[8,17408]{1,0:T(8,128)S(1)} %broadcast_select_fusion.2), channel_id=1, source_target_pairs={{0,240},{4,244},{8,248},{12,252},{16,0},{20,4},{24,8},{28,12},{32,... | collective-permute-start | bytes 1671176 | tf_op jit(solution)/shard_map/ppermute | solution.py:14
  90.1 76.4 %copy-start.24 = (pred[8]{0:T(512)(128)(4,1)S(1)}, pred[8]{0:T(512)(128)(4,1)}, u32[]{:S(2)}) copy-start(pred[8]{0:T(512)(128)(4,1)} %get-tuple-element.125) | copy-start | bytes 28
  92.4 74.3 %copy-start.29 = (s32[8]{0:T(128)S(1)}, s32[8]{0:T(128)}, u32[]{:S(2)}) copy-start(s32[8]{0:T(128)} %get-tuple-element.87) | copy-start | bytes 100
  107.9 78.5 %copy-start.28 = (pred[8]{0:T(512)(128)(4,1)S(1)}, pred[8]{0:T(512)(128)(4,1)}, u32[]{:S(2)}) copy-start(pred[8]{0:T(512)(128)(4,1)} %get-tuple-element.89) | copy-start | bytes 28
  107.9 19.1 %collective-permute-start.3 = (f32[8,17408]{1,0:T(8,128)S(1)}, f32[8,17408]{1,0:T(8,128)S(1)}, u32[]{:S(2)}, u32[]{:S(2)}) collective-permute-start(f32[8,17408]{1,0:T(8,128)S(1)} %broadcast_select_fusion.3), channel_id=1, source_target_pairs={{0,224},{4,228},{8,232},{12,236},{16,240},{20,244},{24,248},{28,25... | collective-permute-start | bytes 1671176 | tf_op jit(solution)/shard_map/ppermute | solution.py:14
  127.1 39.4 %collective-permute-start.4 = (f32[8,17408]{1,0:T(8,128)S(1)}, f32[8,17408]{1,0:T(8,128)S(1)}, u32[]{:S(2)}, u32[]{:S(2)}) collective-permute-start(f32[8,17408]{1,0:T(8,128)S(1)} %broadcast_select_fusion.4), channel_id=1, source_target_pairs={{0,192},{4,196},{8,200},{12,204},{16,208},{20,212},{24,216},{28,22... | collective-permute-start | bytes 1671176 | tf_op jit(solution)/shard_map/ppermute | solution.py:14
  166.5 34.6 %copy-start.23 = (pred[8]{0:T(512)(128)(4,1)S(1)}, pred[8]{0:T(512)(128)(4,1)}, u32[]{:S(2)}) copy-start(pred[8]{0:T(512)(128)(4,1)} %get-tuple-element.86) | copy-start | bytes 28
  166.5 34.7 %copy-start.22 = (f32[1,2048]{1,0:T(1,128)S(1)}, f32[1,2048]{1,0:T(1,128)}, u32[]{:S(2)}) copy-start(f32[1,2048]{1,0:T(1,128)} %copy-done.21) | copy-start | bytes 24580
  166.5 34.7 %copy-start.36 = (bf16[2048,64]{0,1:T(8,128)(2,1)S(1)}, bf16[2048,64]{0,1:T(8,128)(2,1)}, u32[]{:S(2)}) copy-start(bf16[2048,64]{0,1:T(8,128)(2,1)} %param.36) | copy-start | bytes 786436
  166.6 19.7 %collective-permute-start.5 = (f32[8,17408]{1,0:T(8,128)S(1)}, f32[8,17408]{1,0:T(8,128)}, u32[]{:S(2)}, u32[]{:S(2)}) collective-permute-start(f32[8,17408]{1,0:T(8,128)S(1)} %broadcast_select_fusion.5), channel_id=1, source_target_pairs={{0,128},{4,132},{8,136},{12,140},{16,144},{20,148},{24,152},{28,15... | collective-permute-start | bytes 1671176 | tf_op jit(solution)/shard_map/ppermute | solution.py:14
  167.3 34.4 %copy-start.31 = (f32[256]{0:T(256)S(1)}, f32[256]{0:T(256)}, u32[]{:S(2)}) copy-start(f32[256]{0:T(256)} %param.38) | copy-start | bytes 3076
  220.3 46.7 %copy-start.14 = (f32[2048]{0:T(1024)S(1)}, f32[2048]{0:T(1024)}, u32[]{:S(2)}) copy-start(f32[2048]{0:T(1024)} %param.31) | copy-start | bytes 24580
  220.3 46.9 %copy-start.15 = (f32[1,2048]{1,0:T(1,128)S(1)}, f32[1,2048]{1,0:T(1,128)}, u32[]{:S(2)}) copy-start(f32[1,2048]{1,0:T(1,128)} %get-tuple-element.99) | copy-start | bytes 24580
  224.8 72.8 %reduce-scatter.2.cloned.1.call-start = ((), (), s32[]{:S(2)}) async-start(), calls=%async_computation.2 | async-start | bytes 163840 | tf_op jit(solution)/shard_map/reduce_scatter | solution.py:289
  270.5 27.9 %copy-start.32 = (pred[8,4]{1,0:T(8,128)(4,1)S(1)}, pred[8,4]{1,0:T(8,128)(4,1)}, u32[]{:S(2)}) copy-start(pred[8,4]{1,0:T(8,128)(4,1)} %iota_compare_fusion.1) | copy-start | bytes 100
  (22 other events, 168.7 us)
Sparse Core Ops, SparseCore 0:
  225.0 40.6 all-reduce.2
  274.2 23.3 reduce-scatter.1
where the time goes:
time: 309 us; the launch traced here: 306 us
  waiting for transfers between devices  138 us (45%)
  local copies, waits for them, and re-layouts  44.9 us (15%)
  blocking collectives  36.6 us (12%)
  other arithmetic  29.1 us (9%)
  matrix products  27 us (9%)
  between operations  14.9 us (5%)
  starting transfers between devices  14.1 us (5%)
    ppermute x6, waiting for transfers between devices, shifted_2(): return lax.ppermute(value, axis, pairs)  74.9 us
    psum x1, waiting for transfers between devices, on_device(): lax.psum(jnp.dot(flat_heads, attention_exit_projection, preferred_element...  40.4 us
    dynamic_slice x32, local copies, waits for them, and re-layouts, rebuild(): lax.scan(advance, start_state, (jnp.moveaxis(key_rows, 1, 0), jnp.moveaxi...  24.8 us
    reduce_scatter x1, waiting for transfers between devices, on_device(): lax.psum_scatter(lax.dot_general(feedforward_content_proj, flat_hidden, (...  22.9 us
    dot_general x9, matrix products, project(): result = jnp.dot(flat_rows, weight, preferred_element_type=jnp.float32)  15.1 us
    ppermute x6, starting transfers between devices, shifted_2(): return lax.ppermute(value, axis, pairs)  13.8 us
    all_gather x1, blocking collectives, on_device(): lax.all_gather(chosen, 'head', axis=2, tiled=True)  12.6 us
    all_gather x1, blocking collectives, on_device(): lax.all_gather(shift_part.astype(jnp.bfloat16), 'head', axis=2, tiled=True)  12 us
  transfers between devices with their start and end apart: 8, of which 5 were waited for; matrix products, arithmetic and copies ran while one was open for 18% of the time, Pallas kernels for 0%

commit v1 on v0

--- a/solution.py
+++ b/solution.py
@@ -267,11 +267,14 @@
         grouped_layer_scaling,
     )
     flat_heads = grouped_results.reshape(-1, grouped_results.shape[-1])
-    mix_total = lax.psum(
-        jnp.dot(flat_heads, attention_exit_projection, preferred_element_type=jnp.float32).astype(
-            jnp.bfloat16
+    mix_total = jnp.sum(
+        lax.all_gather(
+            jnp.dot(
+                flat_heads, attention_exit_projection, preferred_element_type=jnp.float32
+            ).astype(jnp.bfloat16),
+            "head",
         ),
-        "head",
+        axis=0,
     ).astype(jnp.float32)
     middle = (full_tokens.astype(jnp.float32) + mix_total.reshape(full_tokens.shape)).astype(
         jnp.bfloat16

time: 309 us -> 274 us (0.89)
  waiting for transfers between devices: 138 us -> 91.7 us
  blocking collectives: 36.6 us -> 49.6 us
    psum x1 -> x0, waiting for transfers between devices: 40.4 us -> none  [on_device(): lax.psum(jnp.dot(flat_heads, attention_exit_projection, preferred_element...]
    all_gather x0 -> x1, blocking collectives: none -> 13 us  [on_device(): lax.all_gather(jnp.dot(flat_heads, attention_exit_projection, preferred_e...]
    reduce_scatter x1, waiting for transfers between devices: 22.9 us -> 16.8 us  [on_device(): lax.psum_scatter(lax.dot_general(feedforward_content_proj, flat_hidden, (...]
  transfers between devices with their start and end apart: 8 -> 7, of which waited for: 5 -> 4; matrix products, arithmetic and copies ran while one was open for 18% -> 20% of each run, Pallas kernels for 0% -> 0%
where the time goes in v1:
time: 274 us; the launch traced here: 271 us
  waiting for transfers between devices  91.7 us (33%)
  blocking collectives  49.6 us (18%)
  local copies, waits for them, and re-layouts  44.2 us (16%)
  other arithmetic  28.3 us (10%)
  matrix products  27 us (10%)
  between operations  14.9 us (5%)
  starting transfers between devices  13.9 us (5%)
    ppermute x6, waiting for transfers between devices, shifted_2(): return lax.ppermute(value, axis, pairs)  74.8 us
    dynamic_slice x32, local copies, waits for them, and re-layouts, rebuild(): lax.scan(advance, start_state, (jnp.moveaxis(key_rows, 1, 0), jnp.moveaxi...  24.8 us
    reduce_scatter x1, waiting for transfers between devices, on_device(): lax.psum_scatter(lax.dot_general(feedforward_content_proj, flat_hidden, (...  16.8 us
    dot_general x9, matrix products, project(): result = jnp.dot(flat_rows, weight, preferred_element_type=jnp.float32)  15.1 us
    ppermute x6, starting transfers between devices, shifted_2(): return lax.ppermute(value, axis, pairs)  13.8 us
    all_gather x1, blocking collectives, on_device(): lax.all_gather(jnp.dot(flat_heads, attention_exit_projection, preferred_e...  13 us
    all_gather x1, blocking collectives, on_device(): lax.all_gather(chosen, 'head', axis=2, tiled=True)  12.6 us
    all_gather x1, blocking collectives, on_device(): lax.all_gather(shift_part.astype(jnp.bfloat16), 'head', axis=2, tiled=True)  12 us
  transfers between devices with their start and end apart: 7, of which 4 were waited for; matrix products, arithmetic and copies ran while one was open for 20% of the time, Pallas kernels for 0%

profile of v1, /device:TPU:8, one launch (start us, length us, event | category | flops | bytes accessed | tf_op | source)
XLA Modules:
  0.0 270.7 jit_solution(4720859952503252107)
XLA Ops:
  15.0 12.6 %all_gather.16 = bf16[2,32,2048]{2,1,0:T(8,128)(2,1)S(1)} all-gather(bf16[2,32,512]{2,1,0:T(8,128)(2,1)S(1)} %copy.145), channel_id=1, replica_groups=mesh['grp'=64,'head'=4] {'head'}, dimensions={2}, use_global_device_ids=true | all-gather | bytes 327680 | tf_op jit(solution)/shard_map/all_gather | solution.py:230
  30.2 8.3 %collective-permute-start.1 = (f32[8,17408]{1,0:T(8,128)S(1)}, f32[8,17408]{1,0:T(8,128)}, u32[]{:S(2)}, u32[]{:S(2)}) collective-permute-start(f32[8,17408]{1,0:T(8,128)S(1)} %broadcast_select_fusion.1), channel_id=1, source_target_pairs={{0,248},{4,252},{8,0},{12,4},{16,8},{20,12},{24,16},{28,20},{32,24... | collective-permute-start | bytes 1671176 | tf_op jit(solution)/shard_map/ppermute | solution.py:14
  40.1 2.3 copy.80
  43.9 2.4 convolution_bitcast_fusion.1
  46.3 2.4 convolution_bitcast_fusion
  50.1 5.3 %collective-permute-start.2 = (f32[8,17408]{1,0:T(8,128)S(1)}, f32[8,17408]{1,0:T(8,128)}, u32[]{:S(2)}, u32[]{:S(2)}) collective-permute-start(f32[8,17408]{1,0:T(8,128)S(1)} %broadcast_select_fusion.2), channel_id=1, source_target_pairs={{0,240},{4,244},{8,248},{12,252},{16,0},{20,4},{24,8},{28,12},{32,... | collective-permute-start | bytes 1671176 | tf_op jit(solution)/shard_map/ppermute | solution.py:14
  55.4 34.7 %while.11 = (s32[]{:T(128)}, f32[2,4,64,64]{3,2,1,0:T(8,128)S(1)}, f32[32,2,4,64]{3,2,1,0:T(4,128)S(1)}, f32[32,2,4,64]{3,0,2,1:T(8,128)S(1)}, f32[32,2,4,64]{3,0,2,1:T(8,128)}, /*index=5*/s32[]{:T(128)}, s32[]{:T(128)}) while((s32[]{:T(128)}, f32[2,4,64,64]{3,2,1,0:T(8,128)S(1)}, f32[32,2,4,64]{3,2,1,0:T(4,128)S(1)}, ...), condition=%wide.region_6.7_spmd.clone, body=%wide.region_5.6_spmd.clone.sunk | while | flops 131075 | bytes 280679 | solution.py:97
  92.4 2.3 copy.77
  94.7 12.0 %all_gather.15 = bf16[8,4,2048]{2,1,0:T(4,128)(2,1)S(1)} all-gather(bf16[8,4,512]{2,1,0:T(4,128)(2,1)S(1)} %copy-done.15), channel_id=1, replica_groups=mesh['grp'=64,'head'=4] {'head'}, dimensions={2}, use_global_device_ids=true | all-gather | bytes 163840 | tf_op jit(solution)/shard_map/all_gather | solution.py:229
  108.7 18.2 %collective-permute-done.3 = f32[8,17408]{1,0:T(8,128)S(1)} collective-permute-done((f32[8,17408]{1,0:T(8,128)S(1)}, f32[8,17408]{1,0:T(8,128)S(1)}, u32[]{:S(2)}, u32[]{:S(2)}) %collective-permute-start.3) | collective-permute-done | bytes 557088 | tf_op jit(solution)/shard_map/ppermute | solution.py:14
  128.1 38.4 %collective-permute-done.4 = f32[8,17408]{1,0:T(8,128)S(1)} collective-permute-done((f32[8,17408]{1,0:T(8,128)S(1)}, f32[8,17408]{1,0:T(8,128)S(1)}, u32[]{:S(2)}, u32[]{:S(2)}) %collective-permute-start.4) | collective-permute-done | bytes 557088 | tf_op jit(solution)/shard_map/ppermute | solution.py:14
  168.1 18.2 %collective-permute-done.5 = f32[8,17408]{1,0:T(8,128)} collective-permute-done((f32[8,17408]{1,0:T(8,128)S(1)}, f32[8,17408]{1,0:T(8,128)}, u32[]{:S(2)}, u32[]{:S(2)}) %collective-permute-start.5) | collective-permute-done | bytes 557088 | tf_op jit(solution)/shard_map/ppermute | solution.py:14
  188.4 12.0 %all_gather.17 = bf16[8,2,2048]{2,0,1:T(8,128)(2,1)S(1)} all-gather(bf16[8,2,512]{2,0,1:T(8,128)(2,1)S(1)} %bitcast.195), channel_id=1, replica_groups=mesh['grp'=64,'head'=4] {'head'}, dimensions={2}, use_global_device_ids=true | all-gather | bytes 81920 | tf_op jit(solution)/shard_map/all_gather | solution.py:232
  205.2 1.9 fusion.105
  207.2 1.9 fusion.103
  209.2 1.8 fusion.101
  211.1 4.1 %fusion.36 = (f32[8,4,64,64]{3,2,1,0:T(8,128)}, f32[8,4,64,64]{3,2,1,0:T(8,128)S(1)}) fusion(f32[8,4,64]{2,1,0:T(4,128)S(1)} %copy-done.12, f32[8,4,64]{2,1,0:T(4,128)S(1)} %copy.94, f32[8,4,64]{2,1,0:T(4,128)S(1)} %copy.93, f32[8,4,64]{2,1,0:T(4,128)S(1)} %copy-done.11, f32[8,4,64]{2,1,0:T(4,128)S(1)} %copy.92, f32[8,4,64]{2,1,0:T(4,128)S(1)} %copy.91, ...), kind=kLoop, calls=%fused_computation.49 | loop fusion | flops 2359296 | bytes 2195504 | tf_op jit(solution)/shard_map/jit(_where)/select_n | solution.py:150
  215.2 2.8 %fusion.34 = f32[8,4,1,64]{3,2,1,0:T(1,128)S(1)} fusion(f32[8,4,64]{2,1,0:T(4,128)S(1)} %copy.94, f32[8,4,64]{2,1,0:T(4,128)S(1)} %copy.93, f32[8,4,64]{2,1,0:T(4,128)S(1)} %copy-done.11, f32[8,4,64]{2,1,0:T(4,128)S(1)} %copy.92, f32[8,4,64]{2,1,0:T(4,128)S(1)} %copy.91, f32[4,64]{1,0:T(4,128)S(1)} %copy-done.19, pred[8]{0:T(512)(128)(4,1)S(1)} %copy-done.26, ...), kind=kOutput, calls=%fused_computation.48 | convolution fusion | flops 3538944 | bytes 631832 | tf_op jit(solution)/shard_map/ghl,ghlm->ghm/dot_general | solution.py:142
  218.1 2.3 fusion.30
  220.3 1.7 fusion.26
  224.2 13.0 %all-gather = bf16[128,2048]{1,0:T(8,128)(2,1)S(1)} all-gather(bf16[32,2048]{1,0:T(8,128)(2,1)S(1)} %convolution_convert_fusion.1), channel_id=2, replica_groups=mesh['grp'=64,'head'=4] {'head'}, dimensions={0}, use_global_device_ids=true | all-gather | bytes 655360 | tf_op jit(solution)/shard_map/all_gather | solution.py:271
  238.6 2.7 fusion.10
  241.4 3.4 %fusion.3 = bf16[2048,32]{0,1:T(8,128)(2,1)} fusion(bf16[32,896]{1,0:T(8,128)(2,1)S(1)} %reshape.292, bf16[896,2048]{1,0:T(8,128)(2,1)} %param.43), kind=kOutput, calls=%fused_computation.12 | convolution fusion | flops 117506048 | bytes 3858432 | tf_op jit(solution)/shard_map/dot_general | solution.py:293
  245.5 16.8 %reduce-scatter.2.cloned.1.call-done = bf16[512,32]{0,1:T(8,128)(2,1)} async-done(((bf16[2048,32]{0,1:T(8,128)(2,1)}), bf16[512,32]{0,1:T(8,128)(2,1)}) %reduce-scatter.2.cloned.1.call-update) | async-done | bytes 32784 | tf_op jit(solution)/shard_map/reduce_scatter | solution.py:292
  (273 shorter events, 67.9 us)
Async XLA Ops:
  7.2 216.7 %copy-start = (bf16[256,2048]{1,0:T(8,128)(2,1)S(1)}, bf16[256,2048]{1,0:T(8,128)(2,1)}, u32[]{:S(2)}) copy-start(bf16[256,2048]{1,0:T(8,128)(2,1)} %param.41) | copy-start | bytes 3145732
  7.2 255.2 %reduce-scatter.2.cloned.1.call-start = ((), (), s32[]{:S(2)}) async-start(), calls=%async_computation.1 | async-start | bytes 163840 | tf_op jit(solution)/shard_map/reduce_scatter | solution.py:292
  11.8 26.7 %copy-start.16 = (bf16[64,256]{1,0:T(8,128)(2,1)S(1)}, bf16[64,256]{1,0:T(8,128)(2,1)}, u32[]{:S(2)}) copy-start(bf16[64,256]{1,0:T(8,128)(2,1)} %param.37) | copy-start | bytes 98308
  11.8 26.7 %copy-start.29 = (f32[256]{0:T(256)S(1)}, f32[256]{0:T(256)}, u32[]{:S(2)}) copy-start(f32[256]{0:T(256)} %param.38) | copy-start | bytes 3076
  12.7 15.4 %collective-permute-start = (f32[8,17408]{1,0:T(8,128)}, f32[8,17408]{1,0:T(8,128)S(1)}, u32[]{:S(2)}, u32[]{:S(2)}) collective-permute-start(f32[8,17408]{1,0:T(8,128)} %broadcast_select_fusion), channel_id=1, source_target_pairs={{0,252},{4,0},{8,4},{12,8},{16,12},{20,16},{24,20},{28,24},{32,28}... | collective-permute-start | bytes 1671176 | tf_op jit(solution)/shard_map/ppermute | solution.py:14
  13.5 187.6 %copy-start.18 = (pred[8]{0:T(512)(128)(4,1)}, pred[8]{0:T(512)(128)(4,1)S(1)}, u32[]{:S(2)}) copy-start(pred[8]{0:T(512)(128)(4,1)S(1)} %get-tuple-element.124) | copy-start | bytes 28
  14.7 25.4 %copy-start.20 = (f32[1,2048]{1,0:T(1,128)}, f32[1,2048]{1,0:T(1,128)S(1)}, u32[]{:S(2)}) copy-start(f32[1,2048]{1,0:T(1,128)S(1)} %get-tuple-element.101) | copy-start | bytes 24580
  30.2 18.5 %collective-permute-start.1 = (f32[8,17408]{1,0:T(8,128)S(1)}, f32[8,17408]{1,0:T(8,128)}, u32[]{:S(2)}, u32[]{:S(2)}) collective-permute-start(f32[8,17408]{1,0:T(8,128)S(1)} %broadcast_select_fusion.1), channel_id=1, source_target_pairs={{0,248},{4,252},{8,0},{12,4},{16,8},{20,12},{24,16},{28,20},{32,24... | collective-permute-start | bytes 1671176 | tf_op jit(solution)/shard_map/ppermute | solution.py:14
  48.7 46.0 %copy-start.15 = (bf16[8,4,512]{2,1,0:T(4,128)(2,1)S(1)}, bf16[8,4,512]{2,1,0:T(4,128)(2,1)}, u32[]{:S(2)}) copy-start(bf16[8,4,512]{2,1,0:T(4,128)(2,1)} %param.23) | copy-start | bytes 98308
  48.7 58.0 %copy-start.35 = (s32[8]{0:T(128)S(1)}, s32[8]{0:T(128)}, u32[]{:S(2)}) copy-start(s32[8]{0:T(128)} %param.24) | copy-start | bytes 100
  50.1 58.0 %copy-start.36 = (s32[8]{0:T(128)S(1)}, s32[8]{0:T(128)}, u32[]{:S(2)}) copy-start(s32[8]{0:T(128)} %param.24) | copy-start | bytes 100
  50.1 56.6 %collective-permute-start.2 = (f32[8,17408]{1,0:T(8,128)S(1)}, f32[8,17408]{1,0:T(8,128)}, u32[]{:S(2)}, u32[]{:S(2)}) collective-permute-start(f32[8,17408]{1,0:T(8,128)S(1)} %broadcast_select_fusion.2), channel_id=1, source_target_pairs={{0,240},{4,244},{8,248},{12,252},{16,0},{20,4},{24,8},{28,12},{32,... | collective-permute-start | bytes 1671176 | tf_op jit(solution)/shard_map/ppermute | solution.py:14
  90.1 76.4 %copy-start.23 = (pred[8]{0:T(512)(128)(4,1)S(1)}, pred[8]{0:T(512)(128)(4,1)}, u32[]{:S(2)}) copy-start(pred[8]{0:T(512)(128)(4,1)} %get-tuple-element.125) | copy-start | bytes 28
  92.4 74.3 %copy-start.28 = (s32[8]{0:T(128)S(1)}, s32[8]{0:T(128)}, u32[]{:S(2)}) copy-start(s32[8]{0:T(128)} %get-tuple-element.87) | copy-start | bytes 100
  107.8 78.5 %copy-start.27 = (pred[8]{0:T(512)(128)(4,1)S(1)}, pred[8]{0:T(512)(128)(4,1)}, u32[]{:S(2)}) copy-start(pred[8]{0:T(512)(128)(4,1)} %get-tuple-element.89) | copy-start | bytes 28
  107.8 19.1 %collective-permute-start.3 = (f32[8,17408]{1,0:T(8,128)S(1)}, f32[8,17408]{1,0:T(8,128)S(1)}, u32[]{:S(2)}, u32[]{:S(2)}) collective-permute-start(f32[8,17408]{1,0:T(8,128)S(1)} %broadcast_select_fusion.3), channel_id=1, source_target_pairs={{0,224},{4,228},{8,232},{12,236},{16,240},{20,244},{24,248},{28,25... | collective-permute-start | bytes 1671176 | tf_op jit(solution)/shard_map/ppermute | solution.py:14
  127.1 39.4 %collective-permute-start.4 = (f32[8,17408]{1,0:T(8,128)S(1)}, f32[8,17408]{1,0:T(8,128)S(1)}, u32[]{:S(2)}, u32[]{:S(2)}) collective-permute-start(f32[8,17408]{1,0:T(8,128)S(1)} %broadcast_select_fusion.4), channel_id=1, source_target_pairs={{0,192},{4,196},{8,200},{12,204},{16,208},{20,212},{24,216},{28,22... | collective-permute-start | bytes 1671176 | tf_op jit(solution)/shard_map/ppermute | solution.py:14
  166.4 34.7 %copy-start.22 = (pred[8]{0:T(512)(128)(4,1)S(1)}, pred[8]{0:T(512)(128)(4,1)}, u32[]{:S(2)}) copy-start(pred[8]{0:T(512)(128)(4,1)} %get-tuple-element.86) | copy-start | bytes 28
  166.6 34.7 %copy-start.21 = (f32[1,2048]{1,0:T(1,128)S(1)}, f32[1,2048]{1,0:T(1,128)}, u32[]{:S(2)}) copy-start(f32[1,2048]{1,0:T(1,128)} %copy-done.20) | copy-start | bytes 24580
  166.6 34.7 %copy-start.37 = (bf16[2048,64]{0,1:T(8,128)(2,1)S(1)}, bf16[2048,64]{0,1:T(8,128)(2,1)}, u32[]{:S(2)}) copy-start(bf16[2048,64]{0,1:T(8,128)(2,1)} %param.36) | copy-start | bytes 786436
  166.6 19.7 %collective-permute-start.5 = (f32[8,17408]{1,0:T(8,128)S(1)}, f32[8,17408]{1,0:T(8,128)}, u32[]{:S(2)}, u32[]{:S(2)}) collective-permute-start(f32[8,17408]{1,0:T(8,128)S(1)} %broadcast_select_fusion.5), channel_id=1, source_target_pairs={{0,128},{4,132},{8,136},{12,140},{16,144},{20,148},{24,152},{28,15... | collective-permute-start | bytes 1671176 | tf_op jit(solution)/shard_map/ppermute | solution.py:14
  167.3 34.4 %copy-start.30 = (f32[256]{0:T(256)S(1)}, f32[256]{0:T(256)}, u32[]{:S(2)}) copy-start(f32[256]{0:T(256)} %param.38) | copy-start | bytes 3076
  220.3 17.6 %copy-start.7 = (f32[8,1,2048]{2,1,0:T(1,128)S(1)}, f32[8,1,2048]{2,1,0:T(1,128)}, u32[]{:S(2)}) copy-start(f32[8,1,2048]{2,1,0:T(1,128)} %copy.95) | copy-start | bytes 196612
  241.3 21.8 %copy-start.31 = (pred[8,4]{1,0:T(8,128)(4,1)S(1)}, pred[8,4]{1,0:T(8,128)(4,1)}, u32[]{:S(2)}) copy-start(pred[8,4]{1,0:T(8,128)(4,1)} %iota_compare_fusion.1) | copy-start | bytes 100
  (21 other events, 185.5 us)
Sparse Core Ops, SparseCore 0:
  245.0 17.3 reduce-scatter.1
